TPU v7x, 32 devices: a whole 2x2x4 slice. The times are simulated.
32 devices in a mesh: row: 8 (over y, x, core), col: 4 (over z).
Axes of the slice: x: 2, y: 2, z: 4, core: 2. Of those that a mesh axis runs over, the one named last changes fastest.
Arguments:
- inverse_tiles: float32 [512, 512], P('row', 'col'), may hold values from -0.375 to 0.375
- factor_panels: float32 [3, 512, 256], P(None, 'row', 'col'), may hold values from -6 to 6
- block_rows: int32 [3, 8], replicated, may hold values from 0 to 15, as said below
- couplings: float32 [2, 512, 512], replicated, may hold values from -0.25 to 0.25
Outputs:
- new_columns: float32 [3, 512, 512], P(None, ('row', 'col'))
Inputs may be any that keep to these rules, and one draw needn't show every extreme that they name: `block_rows`: each row lists 8 different row blocks in no particular order; in each row, all 4 blocks q * 4 to q * 4 + 3 of some q are listed.
All inputs are finite; a program needn't handle non-finite values.
Results may differ from a plain program's by a relative error of at most 0.0001.
Values sent between devices are 32-bit elements; how exact they have to be, the bound alone decides.
No kernel may reach another device: no remote copies, remote signals or barrier semaphores. Data moves between devices by JAX's collectives and lax.ppermute only.
A program may use at most 64 MiB of HBM per device.

v0:
```python
import jax
import jax.numpy as jnp
from jax import lax
from jax.sharding import PartitionSpec as P


def on_device(inverse_tiles, factor_panels, block_rows, couplings):
    tile_rows, tile_cols = inverse_tiles.shape
    piece_rows = factor_panels.shape[1]
    listed = block_rows.shape[1]
    col_count = lax.axis_size("col")
    block_size = factor_panels.shape[2] * col_count // listed
    local_blocks = tile_cols // block_size
    my_column = lax.axis_index("col")
    offset = my_column * local_blocks
    targets = offset + jnp.arange(local_blocks, dtype=jnp.int32)
    results = []
    previous = None
    for section in range(factor_panels.shape[0]):
        section_rows = block_rows[section]
        gathered = lax.all_gather(factor_panels[section], "col", axis=1, tiled=True)
        onehot = (section_rows[:, None] == targets[None, :]).astype(jnp.float32)
        picked = jnp.einsum(
            "wpr,pq->wqr",
            gathered.reshape(piece_rows, listed, block_size),
            onehot,
            precision=lax.Precision.HIGHEST,
        ).reshape(piece_rows, tile_cols)
        partial_value = lax.dot_general(
            inverse_tiles,
            lax.all_gather(picked, "row", axis=0, tiled=True),
            (((1,), (1,)), ((), ())),
            precision=lax.Precision.HIGHEST,
            preferred_element_type=jnp.float32,
        )
        summed = lax.psum_scatter(partial_value, "col", scatter_dimension=0, tiled=True)
        if previous is not None:
            summed = summed + jnp.dot(
                previous,
                couplings[section - 1],
                precision=lax.Precision.HIGHEST,
                preferred_element_type=jnp.float32,
            )
        previous = -summed
        results.append(previous)
    return jnp.stack(results)


def solution(mesh):
    return jax.shard_map(
        on_device,
        mesh=mesh,
        in_specs=(P("row", "col"), P(None, "row", "col"), P(), P()),
        out_specs=P(None, ("row", "col"), None),
        check_vma=False,
    )
```

profile of v0, /device:TPU:0, one launch (start us, length us, event | category | flops | bytes accessed | tf_op | source)
XLA Modules:
  0.0 111.6 jit_solution(15987718816973304762)
XLA Ops:
  6.5 0.8 fusion.23
  7.3 0.1 copy.26
  7.4 15.1 %all-gather = f32[1,64,256]{1,2,0:T(8,128)S(1)} all-gather(f32[1,64,64]{1,2,0:T(8,128)S(1)} %copy.26), channel_id=2, replica_groups=mesh['row'=8,'col'=4] {'col'}, dimensions={2}, use_global_device_ids=true | all-gather | bytes 81920 | tf_op jit(solution)/shard_map/all_gather | solution.py:21
  22.5 0.8 slice_bitcast_fusion.2
  23.3 0.3 convolution_bitcast_fusion.5
  23.6 0.1 copy.17
  23.7 9.4 %all_gather.19 = f32[512,128]{1,0:T(8,128)S(1)} all-gather(f32[64,128]{1,0:T(8,128)S(1)} %copy.17), channel_id=1, replica_groups=mesh['row'=8,'col'=4] {'row'}, dimensions={0}, use_global_device_ids=true | all-gather | bytes 294912 | tf_op jit(solution)/shard_map/all_gather | solution.py:31
  33.1 1.1 convolution_bitcast_fusion.2
  34.3 0.1 copy.27
  34.3 13.5 %all-gather.1 = f32[1,64,256]{1,2,0:T(8,128)S(1)} all-gather(f32[1,64,64]{1,2,0:T(8,128)S(1)} %copy.27), channel_id=3, replica_groups=mesh['row'=8,'col'=4] {'col'}, dimensions={2}, use_global_device_ids=true | all-gather | bytes 81920 | tf_op jit(solution)/shard_map/all_gather | solution.py:21
  47.9 0.3 convolution_bitcast_fusion.4
  48.2 0.1 copy.21
  48.2 9.3 %all_gather.21 = f32[512,128]{1,0:T(8,128)S(1)} all-gather(f32[64,128]{1,0:T(8,128)S(1)} %copy.21), channel_id=1, replica_groups=mesh['row'=8,'col'=4] {'row'}, dimensions={0}, use_global_device_ids=true | all-gather | bytes 294912 | tf_op jit(solution)/shard_map/all_gather | solution.py:31
  57.5 1.1 convolution_bitcast_fusion.1
  58.6 0.1 copy.28
  58.7 13.7 %all-gather.2 = f32[1,64,256]{1,2,0:T(8,128)S(1)} all-gather(f32[1,64,64]{1,2,0:T(8,128)S(1)} %copy.28), channel_id=4, replica_groups=mesh['row'=8,'col'=4] {'col'}, dimensions={2}, use_global_device_ids=true | all-gather | bytes 81920 | tf_op jit(solution)/shard_map/all_gather | solution.py:21
  72.4 0.3 convolution_bitcast_fusion.3
  72.8 8.7 %all_gather.23 = f32[512,128]{1,0:T(8,128)S(1)} all-gather(f32[64,128]{1,0:T(8,128)S(1)} %copy.25), channel_id=1, replica_groups=mesh['row'=8,'col'=4] {'row'}, dimensions={0}, use_global_device_ids=true | all-gather | bytes 294912 | tf_op jit(solution)/shard_map/all_gather | solution.py:31
  81.5 1.1 convolution_bitcast_fusion
  82.7 0.8 negate_bitcast_fusion
  83.4 1.4 %fusion.2 = f32[16,512]{1,0:T(8,128)S(1)} fusion(f32[16,512]{1,0:T(8,128)} %reduce-scatter.6.cloned.1.call-done, f32[2,512,512]{2,1,0:T(8,128)S(1)} %copy-done.1, f32[16,512]{1,0:T(8,128)} %reduce-scatter.4.cloned.1.call-done), kind=kOutput, calls=%fused_computation.10 | convolution fusion | flops 50356224 | bytes 1146880 | tf_op jit(solution)/shard_map/dot_general | solution.py:38
  84.8 18.2 %reduce-scatter.8.cloned.1.call-done = f32[16,512]{1,0:T(8,128)} async-done(((f32[64,512]{1,0:T(8,128)}), f32[16,512]{1,0:T(8,128)}) %reduce-scatter.8.cloned.1.call-update) | async-done | bytes 32784 | tf_op jit(solution)/shard_map/reduce_scatter | solution.py:36
  103.0 1.4 %fusion.1 = f32[1,16,512]{2,1,0:T(8,128)S(1)} fusion(f32[16,512]{1,0:T(8,128)} %reduce-scatter.8.cloned.1.call-done, f32[16,512]{1,0:T(8,128)S(1)} %fusion.2, f32[2,512,512]{2,1,0:T(8,128)S(1)} %copy-done.1), kind=kOutput, calls=%fused_computation.8 | convolution fusion | flops 50348032 | bytes 1146880 | tf_op jit(solution)/shard_map/dot_general | solution.py:38
  104.4 0.6 pad_maximum_fusion
  (17 shorter events, 0.3 us)
Async XLA Ops:
  6.5 26.6 %copy-start = (f32[64,128]{1,0:T(8,128)S(1)}, f32[64,128]{1,0:T(8,128)}, u32[]{:S(2)}) copy-start(f32[64,128]{1,0:T(8,128)} %param.4) | copy-start | bytes 98308
  6.5 76.1 %reduce-scatter.4.cloned.1.call-start = ((), (), s32[]{:S(2)}) async-start(), calls=%async_computation.3 | async-start | bytes 163840 | tf_op jit(solution)/shard_map/reduce_scatter | solution.py:36
  23.6 59.9 %copy-start.1 = (f32[2,512,512]{2,1,0:T(8,128)S(1)}, f32[2,512,512]{2,1,0:T(8,128)}, u32[]{:S(2)}) copy-start(f32[2,512,512]{2,1,0:T(8,128)} %param.7) | copy-start | bytes 6291460
  34.2 49.2 %reduce-scatter.6.cloned.1.call-start = ((), (), s32[]{:S(2)}) async-start(), calls=%async_computation.4 | async-start | bytes 163840 | tf_op jit(solution)/shard_map/reduce_scatter | solution.py:36
  58.6 44.4 %reduce-scatter.8.cloned.1.call-start = ((), (), s32[]{:S(2)}) async-start(), calls=%async_computation.5 | async-start | bytes 163840 | tf_op jit(solution)/shard_map/reduce_scatter | solution.py:36
Sparse Core Ops, SparseCore 0:
  34.3 19.9 reduce-scatter.3
  58.7 20.2 reduce-scatter.5
  82.8 20.2 reduce-scatter.7
where the time goes:
time: 112 us
  blocking collectives  69.8 us (62%)
  waiting for transfers between devices  18.3 us (16%)
  between operations  13.2 us (12%)
  matrix products  6.76 us (6%)
  local copies, waits for them, and re-layouts  2.04 us (2%)
  other arithmetic  1.41 us (1%)
    all_gather x3, blocking collectives, on_device(): gathered = lax.all_gather(factor_panels[section], 'col', axis=1, tiled=True)  42.3 us
    all_gather x3, blocking collectives, on_device(): lax.all_gather(picked, 'row', axis=0, tiled=True)  27.5 us
    reduce_scatter x3, waiting for transfers between devices, on_device(): lax.psum_scatter(partial_value, 'col', scatter_dimension=0, tiled=True)  18.2 us
    dot_general x3, matrix products, on_device(): lax.dot_general(inverse_tiles, lax.all_gather(picked, 'row', axis=0, tile...  3.21 us
    dot_general x2, matrix products, on_device(): jnp.dot(previous, couplings[section - 1], precision=lax.Precision.HIGHEST...  2.76 us
  transfers between devices with their start and end apart: 3, of which 1 were waited for; matrix products, arithmetic and copies ran while one was open for 5% of the time, Pallas kernels for 0%

commit v1 on v0

--- a/solution.py
+++ b/solution.py
@@ -2,6 +2,15 @@
 import jax.numpy as jnp
 from jax import lax
 from jax.sharding import PartitionSpec as P
+
+
+def _track_sector(my_data, dim_no):
+    my_data = jnp.moveaxis(my_data, 0, dim_no)
+    carry_out = my_data.shape
+    e_next = my_data.reshape(
+        *carry_out[:dim_no], carry_out[dim_no] * carry_out[dim_no + 1], *carry_out[dim_no + 2 :]
+    )
+    return e_next
 
 
 def on_device(inverse_tiles, factor_panels, block_rows, couplings):
@@ -26,9 +35,22 @@
             onehot,
             precision=lax.Precision.HIGHEST,
         ).reshape(piece_rows, tile_cols)
+
+        def map_wall_on_mesh(slab_in, mesh_ax, dim_k):
+            cores_n = lax.axis_size(mesh_ax)
+            vals = tuple(((w, (w + 1) % cores_n) for w in range(cores_n)))
+            by_rank = [slab_in]
+            while len(by_rank) < cores_n:
+                finding = lax.ppermute(by_rank[-1], mesh_ax, vals)
+                by_rank.append(finding)
+            a_now = lax.axis_index(mesh_ax)
+            by_rank = jnp.stack(by_rank, axis=0)[(a_now - jnp.arange(cores_n)) % cores_n]
+            after = _track_sector(by_rank, dim_k)
+            return after
+
         partial_value = lax.dot_general(
             inverse_tiles,
-            lax.all_gather(picked, "row", axis=0, tiled=True),
+            map_wall_on_mesh(picked, "row", 0),
             (((1,), (1,)), ((), ())),
             precision=lax.Precision.HIGHEST,
             preferred_element_type=jnp.float32,

time: 112 us -> 151 us (1.35)
  waiting for transfers between devices: 18.3 us -> 73.7 us
  blocking collectives: 69.8 us -> 42.2 us
  local copies, waits for them, and re-layouts: 2.04 us -> 11.1 us
  starting transfers between devices: 0.09 us -> 2.03 us
    reduce_scatter x3, waiting for transfers between devices: 18.2 us -> 51.7 us  [on_device(): lax.psum_scatter(partial_value, 'col', scatter_dimension=0, tiled=True)]
    all_gather x3 -> x0, blocking collectives: 27.5 us -> none  [on_device(): lax.all_gather(picked, 'row', axis=0, tiled=True)]
    ppermute x0 -> x21, waiting for transfers between devices: none -> 22 us  [map_wall_on_mesh(): finding = lax.ppermute(by_rank[-1], mesh_ax, vals)]
    unnamed x7 -> x28, local copies, waits for them, and re-layouts: 0.23 us -> 4.67 us
    gather x0 -> x6, local copies, waits for them, and re-layouts: none -> 3.32 us  [map_wall_on_mesh(): jnp.stack(by_rank, axis=0)[(a_now - jnp.arange(cores_n)) % cores_n]]
    ppermute x0 -> x21, starting transfers between devices: none -> 1.94 us  [map_wall_on_mesh(): finding = lax.ppermute(by_rank[-1], mesh_ax, vals)]
  transfers between devices with their start and end apart: 3 -> 24, of which waited for: 1 -> 20; matrix products, arithmetic and copies ran while one was open for 5% -> 10% of each run, Pallas kernels for 0% -> 0%
where the time goes in v1:
time: 151 us
  waiting for transfers between devices  73.7 us (49%)
  blocking collectives  42.2 us (28%)
  between operations  13.3 us (9%)
  local copies, waits for them, and re-layouts  11.1 us (7%)
  matrix products  6.77 us (4%)
  starting transfers between devices  2.03 us (1%)
    reduce_scatter x3, waiting for transfers between devices, on_device(): lax.psum_scatter(partial_value, 'col', scatter_dimension=0, tiled=True)  51.7 us
    all_gather x3, blocking collectives, on_device(): gathered = lax.all_gather(factor_panels[section], 'col', axis=1, tiled=True)  42.2 us
    ppermute x21, waiting for transfers between devices, map_wall_on_mesh(): finding = lax.ppermute(by_rank[-1], mesh_ax, vals)  22 us
    unnamed x28, local copies, waits for them, and re-layouts  4.67 us
    gather x6, local copies, waits for them, and re-layouts, map_wall_on_mesh(): jnp.stack(by_rank, axis=0)[(a_now - jnp.arange(cores_n)) % cores_n]  3.32 us
    dot_general x3, matrix products, on_device(): lax.dot_general(inverse_tiles, map_wall_on_mesh(picked, 'row', 0), (((1,)...  3.21 us
  transfers between devices with their start and end apart: 24, of which 20 were waited for; matrix products, arithmetic and copies ran while one was open for 10% of the time, Pallas kernels for 0%

profile of v1, /device:TPU:0, one launch (start us, length us, event | category | flops | bytes accessed | tf_op | source)
XLA Modules:
  0.0 150.5 jit_solution(3081522991504149923)
XLA Ops:
  7.4 15.1 %all-gather = f32[1,64,256]{1,2,0:T(8,128)S(1)} all-gather(f32[1,64,64]{1,2,0:T(8,128)S(1)} %copy.32), channel_id=2, replica_groups=mesh['row'=8,'col'=4] {'col'}, dimensions={2}, use_global_device_ids=true | all-gather | bytes 81920 | tf_op jit(solution)/shard_map/all_gather | solution.py:30
  23.7 13.6 %all-gather.1 = f32[1,64,256]{1,2,0:T(8,128)S(1)} all-gather(f32[1,64,64]{1,2,0:T(8,128)S(1)} %copy.33), channel_id=3, replica_groups=mesh['row'=8,'col'=4] {'col'}, dimensions={2}, use_global_device_ids=true | all-gather | bytes 81920 | tf_op jit(solution)/shard_map/all_gather | solution.py:30
  37.8 13.5 %all-gather.2 = f32[1,64,256]{1,2,0:T(8,128)S(1)} all-gather(f32[1,64,64]{1,2,0:T(8,128)S(1)} %copy.34), channel_id=4, replica_groups=mesh['row'=8,'col'=4] {'col'}, dimensions={2}, use_global_device_ids=true | all-gather | bytes 81920 | tf_op jit(solution)/shard_map/all_gather | solution.py:30
  52.3 1.6 %collective-permute-start.1 = (f32[64,128]{0,1:T(8,128)S(1)}, f32[64,128]{0,1:T(8,128)S(1)}, u32[]{:S(2)}, u32[]{:S(2)}) collective-permute-start(f32[64,128]{0,1:T(8,128)S(1)} %collective-permute-done), channel_id=1, source_target_pairs={{0,4},{4,8},{8,12},{12,16},{16,20},{20,24},{24,28},{28,0},{1,5},{5... | collective-permute-start | bytes 98312 | tf_op jit(solution)/shard_map/ppermute | solution.py:44
  54.6 1.6 %collective-permute-done.14 = f32[64,128]{0,1:T(8,128)S(1)} collective-permute-done((f32[64,128]{0,1:T(8,128)S(1)}, f32[64,128]{0,1:T(8,128)S(1)}, u32[]{:S(2)}, u32[]{:S(2)}) %collective-permute-start.14) | collective-permute-done | bytes 32800 | tf_op jit(solution)/shard_map/ppermute | solution.py:44
  57.0 1.6 %collective-permute-done.8 = f32[64,128]{0,1:T(8,128)S(1)} collective-permute-done((f32[64,128]{0,1:T(8,128)S(1)}, f32[64,128]{0,1:T(8,128)S(1)}, u32[]{:S(2)}, u32[]{:S(2)}) %collective-permute-start.8) | collective-permute-done | bytes 32800 | tf_op jit(solution)/shard_map/ppermute | solution.py:44
  59.2 1.6 %collective-permute-done.15 = f32[64,128]{0,1:T(8,128)S(1)} collective-permute-done((f32[64,128]{0,1:T(8,128)S(1)}, f32[64,128]{0,1:T(8,128)S(1)}, u32[]{:S(2)}, u32[]{:S(2)}) %collective-permute-start.15) | collective-permute-done | bytes 32800 | tf_op jit(solution)/shard_map/ppermute | solution.py:44
  61.5 1.6 %collective-permute-done.9 = f32[64,128]{0,1:T(8,128)S(1)} collective-permute-done((f32[64,128]{0,1:T(8,128)S(1)}, f32[64,128]{0,1:T(8,128)S(1)}, u32[]{:S(2)}, u32[]{:S(2)}) %collective-permute-start.9) | collective-permute-done | bytes 32800 | tf_op jit(solution)/shard_map/ppermute | solution.py:44
  63.8 1.6 %collective-permute-done.16 = f32[64,128]{0,1:T(8,128)S(1)} collective-permute-done((f32[64,128]{0,1:T(8,128)S(1)}, f32[64,128]{0,1:T(8,128)S(1)}, u32[]{:S(2)}, u32[]{:S(2)}) %collective-permute-start.16) | collective-permute-done | bytes 32800 | tf_op jit(solution)/shard_map/ppermute | solution.py:44
  66.1 1.6 %collective-permute-done.10 = f32[64,128]{0,1:T(8,128)S(1)} collective-permute-done((f32[64,128]{0,1:T(8,128)S(1)}, f32[64,128]{0,1:T(8,128)S(1)}, u32[]{:S(2)}, u32[]{:S(2)}) %collective-permute-start.10) | collective-permute-done | bytes 32800 | tf_op jit(solution)/shard_map/ppermute | solution.py:44
  68.4 1.6 %collective-permute-done.17 = f32[64,128]{0,1:T(8,128)S(1)} collective-permute-done((f32[64,128]{0,1:T(8,128)S(1)}, f32[64,128]{0,1:T(8,128)S(1)}, u32[]{:S(2)}, u32[]{:S(2)}) %collective-permute-start.17) | collective-permute-done | bytes 32800 | tf_op jit(solution)/shard_map/ppermute | solution.py:44
  70.7 1.6 %collective-permute-done.11 = f32[64,128]{0,1:T(8,128)S(1)} collective-permute-done((f32[64,128]{0,1:T(8,128)S(1)}, f32[64,128]{0,1:T(8,128)S(1)}, u32[]{:S(2)}, u32[]{:S(2)}) %collective-permute-start.11) | collective-permute-done | bytes 32800 | tf_op jit(solution)/shard_map/ppermute | solution.py:44
  73.0 1.6 %collective-permute-done.18 = f32[64,128]{0,1:T(8,128)S(1)} collective-permute-done((f32[64,128]{0,1:T(8,128)S(1)}, f32[64,128]{0,1:T(8,128)S(1)}, u32[]{:S(2)}, u32[]{:S(2)}) %collective-permute-start.18) | collective-permute-done | bytes 32800 | tf_op jit(solution)/shard_map/ppermute | solution.py:44
  75.3 1.6 %collective-permute-done.12 = f32[64,128]{0,1:T(8,128)S(1)} collective-permute-done((f32[64,128]{0,1:T(8,128)S(1)}, f32[64,128]{0,1:T(8,128)S(1)}, u32[]{:S(2)}, u32[]{:S(2)}) %collective-permute-start.12) | collective-permute-done | bytes 32800 | tf_op jit(solution)/shard_map/ppermute | solution.py:44
  77.6 1.6 %collective-permute-done.19 = f32[64,128]{0,1:T(8,128)S(1)} collective-permute-done((f32[64,128]{0,1:T(8,128)S(1)}, f32[64,128]{0,1:T(8,128)S(1)}, u32[]{:S(2)}, u32[]{:S(2)}) %collective-permute-start.19) | collective-permute-done | bytes 32800 | tf_op jit(solution)/shard_map/ppermute | solution.py:44
  80.7 1.1 convolution_bitcast_fusion.2
  82.5 1.6 %gather_fusion.1 = f32[8,64,128]{1,2,0:T(8,128)S(1)} fusion(f32[8,64,128]{1,2,0:T(8,128)} %bitcast_dynamic-update-slice_fusion.7, s32[1024]{0:T(1024)S(1)} %pad_clamp_fusion), kind=kCustom, calls=%fused_computation.1 | custom fusion | bytes 524320 | tf_op jit(solution)/shard_map/gather | solution.py:47
  84.3 1.1 convolution_bitcast_fusion.1
  87.1 1.1 convolution_bitcast_fusion
  88.2 14.0 %reduce-scatter.4.cloned.1.call-done = f32[16,512]{1,0:T(8,128)} async-done(((f32[64,512]{1,0:T(8,128)}), f32[16,512]{1,0:T(8,128)}) %reduce-scatter.4.cloned.1.call-update) | async-done | bytes 32784 | tf_op jit(solution)/shard_map/reduce_scatter | solution.py:58
  102.9 19.1 %reduce-scatter.6.cloned.1.call-done = f32[16,512]{1,0:T(8,128)} async-done(((f32[64,512]{1,0:T(8,128)}), f32[16,512]{1,0:T(8,128)}) %reduce-scatter.6.cloned.1.call-update) | async-done | bytes 32784 | tf_op jit(solution)/shard_map/reduce_scatter | solution.py:58
  122.1 1.4 fusion.2
  123.4 18.5 %reduce-scatter.8.cloned.1.call-done = f32[16,512]{1,0:T(8,128)} async-done(((f32[64,512]{1,0:T(8,128)}), f32[16,512]{1,0:T(8,128)}) %reduce-scatter.8.cloned.1.call-update) | async-done | bytes 32784 | tf_op jit(solution)/shard_map/reduce_scatter | solution.py:58
  142.0 1.4 fusion.1
  (85 shorter events, 16.6 us)
Async XLA Ops:
  6.5 95.6 %reduce-scatter.4.cloned.1.call-start = ((), (), s32[]{:S(2)}) async-start(), calls=%async_computation.3 | async-start | bytes 163840 | tf_op jit(solution)/shard_map/reduce_scatter | solution.py:58
  23.6 28.7 %collective-permute-start = (f32[64,128]{0,1:T(8,128)S(1)}, f32[64,128]{0,1:T(8,128)S(1)}, u32[]{:S(2)}, u32[]{:S(2)}) collective-permute-start(f32[64,128]{0,1:T(8,128)S(1)} %bitcast.108), channel_id=1, source_target_pairs={{0,4},{4,8},{8,12},{12,16},{16,20},{20,24},{24,28},{28,0},{1,5},{5... | collective-permute-start | bytes 98312 | tf_op jit(solution)/shard_map/ppermute | solution.py:44
  37.6 16.3 %collective-permute-start.7 = (f32[64,128]{0,1:T(8,128)S(1)}, f32[64,128]{0,1:T(8,128)S(1)}, u32[]{:S(2)}, u32[]{:S(2)}) collective-permute-start(f32[64,128]{0,1:T(8,128)S(1)} %bitcast.110), channel_id=1, source_target_pairs={{0,4},{4,8},{8,12},{12,16},{16,20},{20,24},{24,28},{28,0},{1,5},{5... | collective-permute-start | bytes 98312 | tf_op jit(solution)/shard_map/ppermute | solution.py:44
  51.6 4.6 %collective-permute-start.14 = (f32[64,128]{0,1:T(8,128)S(1)}, f32[64,128]{0,1:T(8,128)S(1)}, u32[]{:S(2)}, u32[]{:S(2)}) collective-permute-start(f32[64,128]{0,1:T(8,128)S(1)} %bitcast.112), channel_id=1, source_target_pairs={{0,4},{4,8},{8,12},{12,16},{16,20},{20,24},{24,28},{28,0},{1,5},{5... | collective-permute-start | bytes 98312 | tf_op jit(solution)/shard_map/ppermute | solution.py:44
  52.3 4.6 %collective-permute-start.1 = (f32[64,128]{0,1:T(8,128)S(1)}, f32[64,128]{0,1:T(8,128)S(1)}, u32[]{:S(2)}, u32[]{:S(2)}) collective-permute-start(f32[64,128]{0,1:T(8,128)S(1)} %collective-permute-done), channel_id=1, source_target_pairs={{0,4},{4,8},{8,12},{12,16},{16,20},{20,24},{24,28},{28,0},{1,5},{5... | collective-permute-start | bytes 98312 | tf_op jit(solution)/shard_map/ppermute | solution.py:44
  53.9 4.6 %collective-permute-start.8 = (f32[64,128]{0,1:T(8,128)S(1)}, f32[64,128]{0,1:T(8,128)S(1)}, u32[]{:S(2)}, u32[]{:S(2)}) collective-permute-start(f32[64,128]{0,1:T(8,128)S(1)} %collective-permute-done.7), channel_id=1, source_target_pairs={{0,4},{4,8},{8,12},{12,16},{16,20},{20,24},{24,28},{28,0},{1,5},{5... | collective-permute-start | bytes 98312 | tf_op jit(solution)/shard_map/ppermute | solution.py:44
  56.2 4.6 %collective-permute-start.15 = (f32[64,128]{0,1:T(8,128)S(1)}, f32[64,128]{0,1:T(8,128)S(1)}, u32[]{:S(2)}, u32[]{:S(2)}) collective-permute-start(f32[64,128]{0,1:T(8,128)S(1)} %collective-permute-done.14), channel_id=1, source_target_pairs={{0,4},{4,8},{8,12},{12,16},{16,20},{20,24},{24,28},{28,0},{1,5},{5... | collective-permute-start | bytes 98312 | tf_op jit(solution)/shard_map/ppermute | solution.py:44
  56.9 4.6 %collective-permute-start.2 = (f32[64,128]{0,1:T(8,128)S(1)}, f32[64,128]{0,1:T(8,128)S(1)}, u32[]{:S(2)}, u32[]{:S(2)}) collective-permute-start(f32[64,128]{0,1:T(8,128)S(1)} %collective-permute-done.1), channel_id=1, source_target_pairs={{0,4},{4,8},{8,12},{12,16},{16,20},{20,24},{24,28},{28,0},{1,5},{5... | collective-permute-start | bytes 98312 | tf_op jit(solution)/shard_map/ppermute | solution.py:44
  58.6 4.6 %collective-permute-start.9 = (f32[64,128]{0,1:T(8,128)S(1)}, f32[64,128]{0,1:T(8,128)S(1)}, u32[]{:S(2)}, u32[]{:S(2)}) collective-permute-start(f32[64,128]{0,1:T(8,128)S(1)} %collective-permute-done.8), channel_id=1, source_target_pairs={{0,4},{4,8},{8,12},{12,16},{16,20},{20,24},{24,28},{28,0},{1,5},{5... | collective-permute-start | bytes 98312 | tf_op jit(solution)/shard_map/ppermute | solution.py:44
  60.8 4.6 %collective-permute-start.16 = (f32[64,128]{0,1:T(8,128)S(1)}, f32[64,128]{0,1:T(8,128)S(1)}, u32[]{:S(2)}, u32[]{:S(2)}) collective-permute-start(f32[64,128]{0,1:T(8,128)S(1)} %collective-permute-done.15), channel_id=1, source_target_pairs={{0,4},{4,8},{8,12},{12,16},{16,20},{20,24},{24,28},{28,0},{1,5},{5... | collective-permute-start | bytes 98312 | tf_op jit(solution)/shard_map/ppermute | solution.py:44
  61.5 4.6 %collective-permute-start.3 = (f32[64,128]{0,1:T(8,128)S(1)}, f32[64,128]{0,1:T(8,128)S(1)}, u32[]{:S(2)}, u32[]{:S(2)}) collective-permute-start(f32[64,128]{0,1:T(8,128)S(1)} %collective-permute-done.2), channel_id=1, source_target_pairs={{0,4},{4,8},{8,12},{12,16},{16,20},{20,24},{24,28},{28,0},{1,5},{5... | collective-permute-start | bytes 98312 | tf_op jit(solution)/shard_map/ppermute | solution.py:44
  63.2 4.6 %collective-permute-start.10 = (f32[64,128]{0,1:T(8,128)S(1)}, f32[64,128]{0,1:T(8,128)S(1)}, u32[]{:S(2)}, u32[]{:S(2)}) collective-permute-start(f32[64,128]{0,1:T(8,128)S(1)} %collective-permute-done.9), channel_id=1, source_target_pairs={{0,4},{4,8},{8,12},{12,16},{16,20},{20,24},{24,28},{28,0},{1,5},{5... | collective-permute-start | bytes 98312 | tf_op jit(solution)/shard_map/ppermute | solution.py:44
  65.4 4.6 %collective-permute-start.17 = (f32[64,128]{0,1:T(8,128)S(1)}, f32[64,128]{0,1:T(8,128)S(1)}, u32[]{:S(2)}, u32[]{:S(2)}) collective-permute-start(f32[64,128]{0,1:T(8,128)S(1)} %collective-permute-done.16), channel_id=1, source_target_pairs={{0,4},{4,8},{8,12},{12,16},{16,20},{20,24},{24,28},{28,0},{1,5},{5... | collective-permute-start | bytes 98312 | tf_op jit(solution)/shard_map/ppermute | solution.py:44
  66.1 4.6 %collective-permute-start.4 = (f32[64,128]{0,1:T(8,128)S(1)}, f32[64,128]{0,1:T(8,128)S(1)}, u32[]{:S(2)}, u32[]{:S(2)}) collective-permute-start(f32[64,128]{0,1:T(8,128)S(1)} %collective-permute-done.3), channel_id=1, source_target_pairs={{0,4},{4,8},{8,12},{12,16},{16,20},{20,24},{24,28},{28,0},{1,5},{5... | collective-permute-start | bytes 98312 | tf_op jit(solution)/shard_map/ppermute | solution.py:44
  67.8 4.6 %collective-permute-start.11 = (f32[64,128]{0,1:T(8,128)S(1)}, f32[64,128]{0,1:T(8,128)S(1)}, u32[]{:S(2)}, u32[]{:S(2)}) collective-permute-start(f32[64,128]{0,1:T(8,128)S(1)} %collective-permute-done.10), channel_id=1, source_target_pairs={{0,4},{4,8},{8,12},{12,16},{16,20},{20,24},{24,28},{28,0},{1,5},{5... | collective-permute-start | bytes 98312 | tf_op jit(solution)/shard_map/ppermute | solution.py:44
  70.0 4.6 %collective-permute-start.18 = (f32[64,128]{0,1:T(8,128)S(1)}, f32[64,128]{0,1:T(8,128)S(1)}, u32[]{:S(2)}, u32[]{:S(2)}) collective-permute-start(f32[64,128]{0,1:T(8,128)S(1)} %collective-permute-done.17), channel_id=1, source_target_pairs={{0,4},{4,8},{8,12},{12,16},{16,20},{20,24},{24,28},{28,0},{1,5},{5... | collective-permute-start | bytes 98312 | tf_op jit(solution)/shard_map/ppermute | solution.py:44
  70.7 4.6 %collective-permute-start.5 = (f32[64,128]{0,1:T(8,128)S(1)}, f32[64,128]{0,1:T(8,128)S(1)}, u32[]{:S(2)}, u32[]{:S(2)}) collective-permute-start(f32[64,128]{0,1:T(8,128)S(1)} %collective-permute-done.4), channel_id=1, source_target_pairs={{0,4},{4,8},{8,12},{12,16},{16,20},{20,24},{24,28},{28,0},{1,5},{5... | collective-permute-start | bytes 98312 | tf_op jit(solution)/shard_map/ppermute | solution.py:44
  72.4 4.6 %collective-permute-start.12 = (f32[64,128]{0,1:T(8,128)S(1)}, f32[64,128]{0,1:T(8,128)S(1)}, u32[]{:S(2)}, u32[]{:S(2)}) collective-permute-start(f32[64,128]{0,1:T(8,128)S(1)} %collective-permute-done.11), channel_id=1, source_target_pairs={{0,4},{4,8},{8,12},{12,16},{16,20},{20,24},{24,28},{28,0},{1,5},{5... | collective-permute-start | bytes 98312 | tf_op jit(solution)/shard_map/ppermute | solution.py:44
  74.6 4.6 %collective-permute-start.19 = (f32[64,128]{0,1:T(8,128)S(1)}, f32[64,128]{0,1:T(8,128)S(1)}, u32[]{:S(2)}, u32[]{:S(2)}) collective-permute-start(f32[64,128]{0,1:T(8,128)S(1)} %collective-permute-done.18), channel_id=1, source_target_pairs={{0,4},{4,8},{8,12},{12,16},{16,20},{20,24},{24,28},{28,0},{1,5},{5... | collective-permute-start | bytes 98312 | tf_op jit(solution)/shard_map/ppermute | solution.py:44
  75.3 4.6 %collective-permute-start.6 = (f32[64,128]{0,1:T(8,128)S(1)}, f32[64,128]{0,1:T(8,128)S(1)}, u32[]{:S(2)}, u32[]{:S(2)}) collective-permute-start(f32[64,128]{0,1:T(8,128)S(1)} %collective-permute-done.5), channel_id=1, source_target_pairs={{0,4},{4,8},{8,12},{12,16},{16,20},{20,24},{24,28},{28,0},{1,5},{5... | collective-permute-start | bytes 98312 | tf_op jit(solution)/shard_map/ppermute | solution.py:44
  76.9 4.9 %collective-permute-start.13 = (f32[64,128]{0,1:T(8,128)S(1)}, f32[64,128]{0,1:T(8,128)S(1)}, u32[]{:S(2)}, u32[]{:S(2)}) collective-permute-start(f32[64,128]{0,1:T(8,128)S(1)} %collective-permute-done.12), channel_id=1, source_target_pairs={{0,4},{4,8},{8,12},{12,16},{16,20},{20,24},{24,28},{28,0},{1,5},{5... | collective-permute-start | bytes 98312 | tf_op jit(solution)/shard_map/ppermute | solution.py:44
  79.1 6.3 %collective-permute-start.20 = (f32[64,128]{0,1:T(8,128)S(1)}, f32[64,128]{0,1:T(8,128)}, u32[]{:S(2)}, u32[]{:S(2)}) collective-permute-start(f32[64,128]{0,1:T(8,128)S(1)} %collective-permute-done.19), channel_id=1, source_target_pairs={{0,4},{4,8},{8,12},{12,16},{16,20},{20,24},{24,28},{28,0},{1,5},{5... | collective-permute-start | bytes 98312 | tf_op jit(solution)/shard_map/ppermute | solution.py:44
  81.8 40.3 %reduce-scatter.6.cloned.1.call-start = ((), (), s32[]{:S(2)}) async-start(), calls=%async_computation.4 | async-start | bytes 163840 | tf_op jit(solution)/shard_map/reduce_scatter | solution.py:58
  85.4 56.6 %reduce-scatter.8.cloned.1.call-start = ((), (), s32[]{:S(2)}) async-start(), calls=%async_computation.5 | async-start | bytes 163840 | tf_op jit(solution)/shard_map/reduce_scatter | solution.py:58
  (2 other events, 114.4 us)
Sparse Core Ops, SparseCore 0:
  81.9 20.1 reduce-scatter.3
  104.4 17.6 reduce-scatter.5
  124.3 17.6 reduce-scatter.7
